TPU v7x, 256 devices: a whole 4x4x8 slice. The times are simulated.
256 devices in a mesh: dp: 4 (over y_lo, core), context: 64 (over y_hi, z, x).
Axes of the slice: x: 4, y: 4 (y_hi: 2, y_lo: 2; y = y_hi * 2 + y_lo), z: 8, core: 2. Of those that a mesh axis runs over, the one named last changes fastest.
Arguments:
- queries: bfloat16 [4, 1024, 8192], P('dp', None, 'context'), may hold values from -6 to 6
- key_stream: bfloat16 [4, 1024, 8192], P('dp', None, 'context'), may hold values from -6 to 6
- value_stream: bfloat16 [4, 1024, 8192], P('dp', None, 'context'), may hold values from -6 to 6
- cotangent: bfloat16 [4, 1024, 8192], P('dp', None, 'context'), may hold values from -6 to 6
- short_taps: float32 [3, 3, 1024], replicated, may hold values from -2 to 2
- residues: float32 [1024, 16], P('context'), may hold values from -1.5 to 1.5
- decay_rates: float32 [1024, 16], P('context'), as said below
Outputs:
- output: bfloat16 [4, 1024, 8192], P('dp', None, 'context')
- adjoint_queries: bfloat16 [4, 1024, 8192], P('dp', None, 'context')
- adjoint_keys: bfloat16 [4, 1024, 8192], P('dp', None, 'context')
- adjoint_values: bfloat16 [4, 1024, 8192], P('dp', None, 'context')
- adjoint_taps: float32 [3, 3, 1024], replicated
- adjoint_residues: float32 [1024, 16], P('context')
- adjoint_decays: float32 [1024, 16], P('context')
Inputs may be any that keep to these rules, and one draw needn't show every extreme that they name: `decay_rates`: every rate lies between 1 / 16384 and 0.05.
All inputs are finite; a program needn't handle non-finite values.
Results may differ from a plain program's by a relative error of at most 0.017.
Values may be sent and summed in bfloat16 or wider, within the bound.
A program may use at most 128 MiB of HBM per device.

v0:
```python
import math
import jax
import jax.numpy as jnp
from jax import lax
from jax.sharding import PartitionSpec as P

HIGHEST_PRECISION = lax.Precision.HIGHEST


def passed_along(x, axis, by):
    peers = lax.axis_size(axis)
    pairs = [(i, i + by) for i in range(peers) if 0 <= i + by < peers]
    return lax.ppermute(x, axis, pairs)


def dft_tables(seq_length):
    total_len = 2 * seq_length
    col_count = min(256, seq_length)
    row_count = total_len // col_count
    half_rows = row_count // 2
    row_index = jnp.arange(row_count, dtype=jnp.int32)
    half_index = jnp.arange(half_rows, dtype=jnp.int32)
    col_index = jnp.arange(col_count, dtype=jnp.int32)
    first_angle = (row_index[:, None] * half_index[None, :] % row_count).astype(jnp.float32) * (
        2.0 * math.pi / row_count
    )
    twist_angle = (row_index[:, None] * col_index[None, :] % total_len).astype(jnp.float32) * (
        2.0 * math.pi / total_len
    )
    second_angle = (col_index[:, None] * col_index[None, :] % col_count).astype(jnp.float32) * (
        2.0 * math.pi / col_count
    )
    return (
        jnp.cos(first_angle),
        jnp.sin(first_angle),
        jnp.cos(twist_angle),
        jnp.sin(twist_angle),
        jnp.cos(second_angle),
        jnp.sin(second_angle),
    )


def along_cols(array, table):
    return jnp.einsum("bckm,mj->bckj", array, table, precision=HIGHEST_PRECISION)


def forward_dft(signal, tables):
    cos_first, sin_first, cos_twist, sin_twist, cos_second, sin_second = tables
    batch_here, chan_here, seq_length = signal.shape
    folded = signal.reshape(batch_here, chan_here, cos_first.shape[1], cos_second.shape[0])
    part_re = jnp.einsum("kn,bcnm->bckm", cos_first, folded, precision=HIGHEST_PRECISION)
    part_im = -jnp.einsum("kn,bcnm->bckm", sin_first, folded, precision=HIGHEST_PRECISION)
    twist_re = part_re * cos_twist + part_im * sin_twist
    twist_im = part_im * cos_twist - part_re * sin_twist
    spec_re = along_cols(twist_re, cos_second) + along_cols(twist_im, sin_second)
    spec_im = along_cols(twist_im, cos_second) - along_cols(twist_re, sin_second)
    return (spec_re, spec_im)


def inverse_dft(spec_re, spec_im, tables):
    cos_first, sin_first, cos_twist, sin_twist, cos_second, sin_second = tables
    back_re = along_cols(spec_re, cos_second) - along_cols(spec_im, sin_second)
    back_im = along_cols(spec_im, cos_second) + along_cols(spec_re, sin_second)
    turn_re = back_re * cos_twist - back_im * sin_twist
    turn_im = back_im * cos_twist + back_re * sin_twist
    folded = jnp.einsum(
        "kn,bckm->bcnm", cos_first, turn_re, precision=HIGHEST_PRECISION
    ) - jnp.einsum("kn,bckm->bcnm", sin_first, turn_im, precision=HIGHEST_PRECISION)
    batch_here, chan_here, half_rows, col_count = folded.shape
    return folded.reshape(batch_here, chan_here, half_rows * col_count) / (
        2.0 * half_rows * col_count
    )


def freq_grid(seq_length, tables):
    row_count = tables[2].shape[0]
    col_count = tables[2].shape[1]
    total_len = 2 * seq_length
    freq_index = (
        jnp.arange(row_count, dtype=jnp.int32)[:, None]
        + row_count * jnp.arange(col_count, dtype=jnp.int32)[None, :]
    )
    signed_index = jnp.where(freq_index >= seq_length, freq_index - total_len, freq_index)
    angle = signed_index.astype(jnp.float32) * (2.0 * math.pi / total_len)
    half_sine = jnp.sin(0.5 * angle)
    return (half_sine * half_sine, jnp.sin(angle), freq_index % 2 == 0)


def mode_response(decay, half_square, sine, is_even, seq_length):
    damping = jnp.exp(-decay)
    amplitude = jnp.sqrt(-jnp.expm1(-2.0 * decay))
    numerator = jnp.where(
        is_even, -jnp.expm1(-decay * seq_length), 1.0 + jnp.exp(-decay * seq_length)
    )
    real_den = -jnp.expm1(-decay) + 2.0 * damping * half_square
    imag_den = damping * sine
    factor = amplitude * numerator / (real_den * real_den + imag_den * imag_den)
    return (factor * real_den, -factor * imag_den)


def filter_spectrum(residues, decay_rates, grid, seq_length):
    half_square, sine, is_even = grid

    def add_mode(carry, inputs):
        residue_col, decay_col = inputs
        resp_re, resp_im = mode_response(
            decay_col[:, None, None], half_square, sine, is_even, seq_length
        )
        weight_col = residue_col[:, None, None]
        return ((carry[0] + weight_col * resp_re, carry[1] + weight_col * resp_im), None)

    empty = jnp.zeros((residues.shape[0],) + sine.shape, jnp.float32)
    spectra, unused = lax.scan(add_mode, (empty, empty), (residues.T, decay_rates.T))
    return spectra


def mode_adjoints(residues, decay_rates, adj_re, adj_im, grid, seq_length):
    half_square, sine, is_even = grid

    def one_mode(carry, inputs):
        residue_col, decay_col = inputs
        decay_cube = decay_col[:, None, None]

        def response(decay_value):
            return mode_response(decay_value, half_square, sine, is_even, seq_length)

        values, tangents = jax.jvp(response, (decay_cube,), (jnp.ones_like(decay_cube),))
        residue_term = jnp.sum(adj_re * values[0] + adj_im * values[1], axis=(1, 2))
        decay_term = (
            jnp.sum(adj_re * tangents[0] + adj_im * tangents[1], axis=(1, 2))
            * residue_col
            * decay_col
        )
        return (carry, (residue_term, decay_term))

    unused, terms = lax.scan(one_mode, jnp.zeros((), jnp.float32), (residues.T, decay_rates.T))
    return (terms[0].T, terms[1].T)


def owner_work(gated, upstream, residues, decay_rates):
    seq_length = gated.shape[2]
    tables = dft_tables(seq_length)
    grid = freq_grid(seq_length, tables)
    spec_re, spec_im = filter_spectrum(residues, decay_rates, grid, seq_length)

    def convolve(signal, filt_re, filt_im):
        sig_re, sig_im = forward_dft(signal, tables)
        return inverse_dft(
            sig_re * filt_re - sig_im * filt_im, sig_re * filt_im + sig_im * filt_re, tables
        )

    mixed_exact, pullback = jax.vjp(convolve, gated.astype(jnp.float32), spec_re, spec_im)
    source_adj, adj_re, adj_im = pullback(upstream.astype(jnp.float32))
    residue_adj, decay_adj = mode_adjoints(residues, decay_rates, adj_re, adj_im, grid, seq_length)
    return (
        mixed_exact.astype(jnp.bfloat16),
        source_adj.astype(jnp.bfloat16),
        residue_adj,
        decay_adj,
    )


def featurize(extended, weights, length_here):
    reach_back = weights.shape[0] - 1
    result = jnp.zeros(extended[:, :, :length_here].shape, jnp.float32)
    for offset in range(reach_back + 1):
        start_at = reach_back - offset
        result = (
            result
            + weights[offset][None, :, None] * extended[:, :, start_at : start_at + length_here]
        )
    return result


def per_device(queries, key_stream, value_stream, cotangent, short_taps, residues, decay_rates):
    reach_back = short_taps.shape[1] - 1
    length_here = queries.shape[2]
    rim_parts = passed_along(
        (
            queries[:, :, length_here - reach_back :],
            key_stream[:, :, length_here - reach_back :],
            value_stream[:, :, length_here - reach_back :],
        ),
        "context",
        1,
    )
    extended = [
        jnp.concatenate([rim_part, signal], axis=2).astype(jnp.float32)
        for signal, rim_part in zip((queries, key_stream, value_stream), rim_parts)
    ]
    query_short, key_short, value_short = [
        featurize(extended[stream], short_taps[stream], length_here).astype(jnp.bfloat16)
        for stream in range(3)
    ]
    upstream = (cotangent.astype(jnp.float32) * query_short.astype(jnp.float32)).astype(
        jnp.bfloat16
    )
    key_own, value_own, upstream_own = (
        lax.all_to_all(key_short, "context", split_axis=1, concat_axis=2, tiled=True),
        lax.all_to_all(value_short, "context", split_axis=1, concat_axis=2, tiled=True),
        lax.all_to_all(upstream, "context", split_axis=1, concat_axis=2, tiled=True),
    )
    gated_own = (key_own.astype(jnp.float32) * value_own.astype(jnp.float32)).astype(jnp.bfloat16)
    mixed_own, source_own, residue_adj, decay_adj = owner_work(
        gated_own, upstream_own, residues, decay_rates
    )
    key_adj_own = (source_own.astype(jnp.float32) * value_own.astype(jnp.float32)).astype(
        jnp.bfloat16
    )
    value_adj_own = (source_own.astype(jnp.float32) * key_own.astype(jnp.float32)).astype(
        jnp.bfloat16
    )
    mixed_seq, key_adj, value_adj = (
        lax.all_to_all(mixed_own, "context", split_axis=2, concat_axis=1, tiled=True),
        lax.all_to_all(key_adj_own, "context", split_axis=2, concat_axis=1, tiled=True),
        lax.all_to_all(value_adj_own, "context", split_axis=2, concat_axis=1, tiled=True),
    )
    output = (query_short.astype(jnp.float32) * mixed_seq.astype(jnp.float32)).astype(jnp.bfloat16)
    query_adj = (cotangent.astype(jnp.float32) * mixed_seq.astype(jnp.float32)).astype(jnp.bfloat16)
    stream_adjs = (query_adj, key_adj, value_adj)
    next_parts = passed_along(
        (query_adj[:, :, :reach_back], key_adj[:, :, :reach_back], value_adj[:, :, :reach_back]),
        "context",
        -1,
    )
    signal_adjs = []
    tap_rows = []
    for stream in range(3):
        adjoint_f = stream_adjs[stream].astype(jnp.float32)
        ahead = jnp.concatenate([stream_adjs[stream], next_parts[stream]], axis=2).astype(
            jnp.float32
        )
        total_adj = jnp.zeros(adjoint_f.shape, jnp.float32)
        per_tap = []
        for offset in range(reach_back + 1):
            total_adj = (
                total_adj
                + short_taps[stream, offset][None, :, None]
                * ahead[:, :, offset : offset + length_here]
            )
            start_at = reach_back - offset
            per_tap.append(
                jnp.sum(
                    adjoint_f * extended[stream][:, :, start_at : start_at + length_here],
                    axis=(0, 2),
                )
            )
        signal_adjs.append(total_adj.astype(jnp.bfloat16))
        tap_rows.append(jnp.stack(per_tap))
    tap_part = jnp.stack(tap_rows)
    token_scale = 1.0 / math.sqrt(
        queries.shape[0] * lax.axis_size("dp") * length_here * lax.axis_size("context")
    )
    tap_total = lax.psum(tap_part, ("dp", "context"))
    residue_own, decay_own = lax.psum((residue_adj, decay_adj), "dp")
    return (
        output,
        signal_adjs[0],
        signal_adjs[1],
        signal_adjs[2],
        tap_total * token_scale,
        residue_own * token_scale,
        decay_own * token_scale,
    )


def solution(mesh):
    in_specs = (
        P("dp", None, "context"),
        P("dp", None, "context"),
        P("dp", None, "context"),
        P("dp", None, "context"),
        P(),
        P("context", None),
        P("context", None),
    )
    out_specs = (
        P("dp", None, "context"),
        P("dp", None, "context"),
        P("dp", None, "context"),
        P("dp", None, "context"),
        P(),
        P("context", None),
        P("context", None),
    )
    return jax.shard_map(
        per_device, mesh=mesh, in_specs=in_specs, out_specs=out_specs, check_vma=False
    )
```

profile of v0, /device:TPU:230, one launch (start us, length us, event | category | flops | bytes accessed | tf_op | source)
XLA Modules:
  0.0 640.2 jit_solution(5047321556675018098)
XLA Ops:
  4.7 7.0 %collective-permute-done.1 = bf16[1,1024,2]{2,1,0:T(8,128)(2,1)S(1)} collective-permute-done((bf16[1,1024,2]{2,1,0:T(8,128)(2,1)S(1)}, bf16[1,1024,2]{2,1,0:T(8,128)(2,1)S(1)}, u32[]{:S(2)}, u32[]{:S(2)}) %collective-permute-start.1) | collective-permute-done | bytes 4128 | tf_op jit(solution)/shard_map/ppermute | solution.py:13
  15.7 2.2 reduce
  18.7 12.4 %all-to-all-start = ((bf16[64,2,1024]{2,1,0:T(2,128)(2,1)}), bf16[64,2,1024]{2,1,0:T(2,128)(2,1)S(1)}, u32[]{:S(2)}, u32[]{:S(2)}) async-start(bf16[64,2,1024]{2,1,0:T(2,128)(2,1)} %reshape.877), calls=%async_computation | async-start | bytes 524288 | tf_op jit(solution)/shard_map/all_to_all | solution.py:199
  31.3 4.9 collective-permute-start.2
  37.1 3.4 collective-permute-start
  44.2 2.3 reduce.1
  47.2 13.0 %all-to-all-start.1 = ((bf16[64,2,1024]{2,1,0:T(2,128)(2,1)}), bf16[64,2,1024]{2,1,0:T(2,128)(2,1)S(1)}, u32[]{:S(2)}, u32[]{:S(2)}) async-start(bf16[64,2,1024]{2,1,0:T(2,128)(2,1)} %reshape.879), calls=%async_computation.1 | async-start | bytes 524288 | tf_op jit(solution)/shard_map/all_to_all | solution.py:200
  60.3 47.8 %while.33 = (s32[]{:T(128)}, f32[16,64,256]{2,1,0:T(8,128)S(1)}, f32[16,64,256]{2,1,0:T(8,128)S(1)}, f32[16,16]{1,0:T(8,128)}, f32[16,16]{1,0:T(8,128)}, /*index=5*/s32[256]{0:T(256)S(1)}, s32[]{:T(128)}, s32[]{:T(128)}) while((s32[]{:T(128)}, f32[16,64,256]{2,1,0:T(8,128)S(1)}, ...), condition=%wide.region_1.2_spmd.clone.clone.clone, body=%wide.region_0.1_spmd.clone.clone.clone.sunk | while | flops 5062803 | bytes 4492583 | solution.py:113
  113.7 2.3 reduce.2
  116.8 13.0 %all-to-all-start.3 = ((bf16[64,2,1024]{2,1,0:T(2,128)(2,1)}), bf16[64,2,1024]{2,1,0:T(2,128)(2,1)}, u32[]{:S(2)}, u32[]{:S(2)}) async-start(bf16[64,2,1024]{2,1,0:T(2,128)(2,1)} %reshape.883), calls=%async_computation.3 | async-start | bytes 524288 | tf_op jit(solution)/shard_map/all_to_all | solution.py:201
  134.9 4.8 all-to-all-done.3
  139.7 3.1 reshape.884
  149.5 2.2 convolution_bitcast_fusion.1
  166.0 3.9 multiply_add_fusion.3
  169.9 3.0 fusion.132
  172.9 3.2 fusion.77
  187.7 6.7 %copy.214 = bf16[1,16,8192]{1,0,2:T(2,128)(2,1)} copy(bf16[1,16,8192]{2,1,0:T(8,128)(2,1)S(1)} %convert_element_type.446) | data formatting | bytes 524288 | tf_op jit(solution)/shard_map/convert_element_type | solution.py:156
  194.4 47.1 %reduce.3 = bf16[8192,16]{1,0:T(8,128)(2,1)} reduce(bf16[8192,1,16]{2,1,0:T(2,128)(2,1)} %bitcast.310, bf16[]{:T(256)} %broadcast.596), dimensions={1}, to_apply=%bitcast.253.reduce_sub_computation | reduce | bytes 524290
  241.5 4.4 reshape.881
  245.9 8.5 %all-to-all-start.2 = ((bf16[64,2,1024]{2,1,0:T(2,128)(2,1)}), bf16[64,2,1024]{2,1,0:T(2,128)(2,1)S(1)}, u32[]{:S(2)}, u32[]{:S(2)}) async-start(bf16[64,2,1024]{2,1,0:T(2,128)(2,1)} %reshape.881), calls=%async_computation.2 | async-start | bytes 524288 | tf_op jit(solution)/shard_map/all_to_all | solution.py:214
  254.4 3.2 convolution_add_fusion.1
  257.6 3.2 convolution_add_fusion
  262.7 2.7 copy.231
  265.3 2.6 copy.221
  267.9 2.6 copy.225
  270.6 9.7 %multiply_convert_fusion = (bf16[1,16,8192]{1,0,2:T(2,128)(2,1)}, bf16[1,16,8192]{1,0,2:T(2,128)(2,1)}) fusion(f32[1,16,8192]{1,0,2:T(1,128)} %bitcast.306, f32[1,16,8192]{1,0,2:T(1,128)} %bitcast.308, f32[1,16,8192]{1,0,2:T(1,128)} %bitcast.307), kind=kLoop, calls=%fused_computation.90 | loop fusion | flops 524288 | bytes 2097152 | tf_op jit(solution)/shard_map/convert_element_type | solution.py:210
  280.3 46.9 %reduce.4 = bf16[8192,16]{1,0:T(8,128)(2,1)} reduce(bf16[8192,1,16]{2,1,0:T(2,128)(2,1)} %bitcast.309, bf16[]{:T(256)} %broadcast.596), dimensions={1}, to_apply=%bitcast.257.reduce_sub_computation | reduce | bytes 524290
  327.2 4.4 reshape.885
  331.6 13.4 %all-to-all-start.4 = ((bf16[64,2,1024]{2,1,0:T(2,128)(2,1)}), bf16[64,2,1024]{2,1,0:T(2,128)(2,1)}, u32[]{:S(2)}, u32[]{:S(2)}) async-start(bf16[64,2,1024]{2,1,0:T(2,128)(2,1)} %reshape.885), calls=%async_computation.4 | async-start | bytes 524288 | tf_op jit(solution)/shard_map/all_to_all | solution.py:215
  345.1 67.6 %while.32 = (s32[]{:T(128)}, f32[16,16]{1,0:T(8,128)S(1)}, f32[16,16]{1,0:T(8,128)S(1)}, f32[16,16]{1,0:T(8,128)}, f32[16,64,256]{2,1,0:T(8,128)S(1)}, /*index=5...) while((s32[]{:T(128)}, f32[16,16]{1,0:T(8,128)S(1)}, ...), condition=%wide.region_15.16_spmd.clone.clone.clone, body=%wide.region_12.15_spmd.clone.clone.clone.sunk | while | flops 12403026 | bytes 2396661 | solution.py:136
  359.0 2.2 fusion.310
  384.4 2.2 fusion.310
  412.8 45.3 %reduce.5 = bf16[8192,16]{1,0:T(8,128)(2,1)S(1)} reduce(bf16[8192,1,16]{2,1,0:T(2,128)(2,1)} %bitcast.305, bf16[]{:T(256)} %broadcast.596), dimensions={1}, to_apply=%bitcast.259.reduce_sub_computation | reduce | bytes 524290
  458.1 2.9 reshape.887
  461.0 10.4 %all-reduce = (f32[16,16]{1,0:T(8,128)S(1)}, f32[16,16]{1,0:T(8,128)S(1)}) all-reduce(f32[16,16]{1,0:T(8,128)S(1)} %bitcast.355, f32[16,16]{1,0:T(8,128)S(1)} %bitcast.356), channel_id=1, replica_groups=mesh['dp'=4,'context'=64] {'dp'}, use_global_device_ids=true, to_apply=%region_16.17 | all-reduce | flops 512 | bytes 4096 | tf_op jit(solution)/shard_map/psum | solution.py:255
  472.6 7.6 %reshape.882 = bf16[8192,1,16]{2,1,0:T(2,128)(2,1)} reshape(bf16[64,2,1024]{2,1,0:T(2,128)(2,1)S(1)} %all-to-all-done.2) | data formatting | bytes 524288
  480.2 7.9 %copy.215 = bf16[1,16,8192]{2,1,0:T(8,128)(2,1)S(1)} copy(bf16[1,16,8192]{1,0,2:T(2,128)(2,1)} %bitcast.311) | data formatting | bytes 524288 | tf_op jit(solution)/shard_map/all_to_all | solution.py:214
  488.1 13.0 %all-to-all-start.5 = ((bf16[64,2,1024]{2,1,0:T(2,128)(2,1)}), bf16[64,2,1024]{2,1,0:T(2,128)(2,1)S(1)}, u32[]{:S(2)}, u32[]{:S(2)}) async-start(bf16[64,2,1024]{2,1,0:T(2,128)(2,1)} %reshape.887), calls=%async_computation.5 | async-start | bytes 524288 | tf_op jit(solution)/shard_map/all_to_all | solution.py:216
  501.6 9.9 %reshape.886 = bf16[8192,1,16]{2,1,0:T(2,128)(2,1)} reshape(bf16[64,2,1024]{2,1,0:T(2,128)(2,1)} %all-to-all-done.4) | data formatting | bytes 524288
  511.4 7.9 %copy.223 = bf16[1,16,8192]{2,1,0:T(8,128)(2,1)S(1)} copy(bf16[1,16,8192]{1,0,2:T(2,128)(2,1)} %bitcast.312) | data formatting | bytes 524288 | tf_op jit(solution)/shard_map/all_to_all | solution.py:215
  520.3 7.6 %reshape.888 = bf16[8192,1,16]{2,1,0:T(2,128)(2,1)} reshape(bf16[64,2,1024]{2,1,0:T(2,128)(2,1)S(1)} %all-to-all-done.5) | data formatting | bytes 524288
  528.0 8.0 %copy.227 = bf16[1,16,8192]{2,1,0:T(8,128)(2,1)S(1)} copy(bf16[1,16,8192]{1,0,2:T(2,128)(2,1)} %bitcast.313) | data formatting | bytes 524288 | tf_op jit(solution)/shard_map/all_to_all | solution.py:216
  537.1 2.5 fusion.91
  539.6 75.4 %psum.21 = f32[3,3,1024]{2,1,0:T(4,128)S(1)} all-reduce(f32[3,3,1024]{2,1,0:T(4,128)S(1)} %pad_maximum_fusion), channel_id=1, replica_groups=mesh['dp'=4,'context'=64] {'dp','context'}, use_global_device_ids=true, to_apply=%region_11.12 | all-reduce | flops 9216 | bytes 73728 | tf_op jit(solution)/shard_map/psum | solution.py:254
  617.6 3.3 collective-permute-start.4
  621.1 2.6 collective-permute-start.3
  623.7 8.1 %collective-permute-done.5 = bf16[1,1024,2]{2,1,0:T(8,128)(2,1)S(1)} collective-permute-done((bf16[1,1024,2]{2,1,0:T(8,128)(2,1)S(1)}, bf16[1,1024,2]{2,1,0:T(8,128)(2,1)S(1)}, u32[]{:S(2)}, u32[]{:S(2)}) %collective-permute-start.5) | collective-permute-done | bytes 4128 | tf_op jit(solution)/shard_map/ppermute | solution.py:13
  633.4 3.0 collective-permute-done.4
  (406 shorter events, 180.8 us)
Async XLA Ops:
  0.6 30.5 %copy-start.19 = (bf16[1,1024,128]{2,1,0:T(8,128)(2,1)S(1)}, bf16[1,1024,128]{2,1,0:T(8,128)(2,1)}, u32[]{:S(2)}) copy-start(bf16[1,1024,128]{2,1,0:T(8,128)(2,1)} %param.13) | copy-start | bytes 786436
  0.6 35.5 %copy-start.20 = (bf16[1,1024,128]{2,1,0:T(8,128)(2,1)S(1)}, bf16[1,1024,128]{2,1,0:T(8,128)(2,1)}, u32[]{:S(2)}) copy-start(bf16[1,1024,128]{2,1,0:T(8,128)(2,1)} %param.11) | copy-start | bytes 786436
  0.7 39.8 %copy-start.33 = (f32[16,16]{1,0:T(8,128)S(1)}, f32[16,16]{1,0:T(8,128)}, u32[]{:S(2)}) copy-start(f32[16,16]{1,0:T(8,128)} %param.16) | copy-start | bytes 3076
  0.7 40.5 %copy-start.34 = (f32[16,16]{1,0:T(8,128)S(1)}, f32[16,16]{1,0:T(8,128)}, u32[]{:S(2)}) copy-start(f32[16,16]{1,0:T(8,128)} %param.17) | copy-start | bytes 3076
  1.8 9.9 %collective-permute-start.1 = (bf16[1,1024,2]{2,1,0:T(8,128)(2,1)S(1)}, bf16[1,1024,2]{2,1,0:T(8,128)(2,1)S(1)}, u32[]{:S(2)}, u32[]{:S(2)}) collective-permute-start(bf16[1,1024,2]{2,1,0:T(8,128)(2,1)S(1)} %slice.146), channel_id=1, source_target_pairs={{0,1},{1,2},{2,3},{3,4},{4,5},{5,6},{6,7},{7,8},{8,9},{9,10},{10,1... | collective-permute-start | bytes 12296 | tf_op jit(solution)/shard_map/ppermute | solution.py:13
  4.7 26.4 %copy-start.21 = (f32[1,1,1024]{2,1,0:T(1,128)}, f32[1,1,1024]{2,1,0:T(1,128)S(1)}, u32[]{:S(2)}) copy-start(f32[1,1,1024]{2,1,0:T(1,128)S(1)} %get-tuple-element.452) | copy-start | bytes 12292
  4.7 26.4 %copy-start.23 = (f32[1,1,1024]{2,1,0:T(1,128)}, f32[1,1,1024]{2,1,0:T(1,128)S(1)}, u32[]{:S(2)}) copy-start(f32[1,1,1024]{2,1,0:T(1,128)S(1)} %get-tuple-element.453) | copy-start | bytes 12292
  4.7 26.4 %copy-start.25 = (f32[1,1,1024]{2,1,0:T(1,128)}, f32[1,1,1024]{2,1,0:T(1,128)S(1)}, u32[]{:S(2)}) copy-start(f32[1,1,1024]{2,1,0:T(1,128)S(1)} %get-tuple-element.454) | copy-start | bytes 12292
  4.7 37.4 %copy-start.27 = (f32[1,1,1024]{2,1,0:T(1,128)}, f32[1,1,1024]{2,1,0:T(1,128)S(1)}, u32[]{:S(2)}) copy-start(f32[1,1,1024]{2,1,0:T(1,128)S(1)} %get-tuple-element.451) | copy-start | bytes 12292
  4.7 37.4 %copy-start.29 = (f32[1,1,1024]{2,1,0:T(1,128)}, f32[1,1,1024]{2,1,0:T(1,128)S(1)}, u32[]{:S(2)}) copy-start(f32[1,1,1024]{2,1,0:T(1,128)S(1)} %get-tuple-element.458) | copy-start | bytes 12292
  4.7 37.4 %copy-start.31 = (f32[1,1,1024]{2,1,0:T(1,128)}, f32[1,1,1024]{2,1,0:T(1,128)S(1)}, u32[]{:S(2)}) copy-start(f32[1,1,1024]{2,1,0:T(1,128)S(1)} %get-tuple-element.459) | copy-start | bytes 12292
  12.9 1.0 copy-start.4
  18.7 28.5 %all-to-all-start = ((bf16[64,2,1024]{2,1,0:T(2,128)(2,1)}), bf16[64,2,1024]{2,1,0:T(2,128)(2,1)S(1)}, u32[]{:S(2)}, u32[]{:S(2)}) async-start(bf16[64,2,1024]{2,1,0:T(2,128)(2,1)} %reshape.877), calls=%async_computation | async-start | bytes 524288 | tf_op jit(solution)/shard_map/all_to_all | solution.py:199
  31.3 10.5 %collective-permute-start.2 = (bf16[1,1024,2]{2,1,0:T(8,128)(2,1)S(1)}, bf16[1,1024,2]{2,1,0:T(8,128)(2,1)S(1)}, u32[]{:S(2)}, u32[]{:S(2)}) collective-permute-start(bf16[1,1024,2]{2,1,0:T(8,128)(2,1)S(1)} %slice.153), channel_id=1, source_target_pairs={{0,1},{1,2},{2,3},{3,4},{4,5},{5,6},{6,7},{7,8},{8,9},{9,10},{10,1... | collective-permute-start | bytes 12296 | tf_op jit(solution)/shard_map/ppermute | solution.py:13
  37.1 71.1 %collective-permute-start = (bf16[1,1024,2]{1,2,0:T(2,128)(2,1)}, bf16[1,1024,2]{1,2,0:T(2,128)(2,1)}, u32[]{:S(2)}, u32[]{:S(2)}) collective-permute-start(bf16[1,1024,2]{1,2,0:T(2,128)(2,1)} %copy.232), channel_id=1, source_target_pairs={{0,1},{1,2},{2,3},{3,4},{4,5},{5,6},{6,7},{7,8},{8,9},{9,10},{10,1... | collective-permute-start | bytes 12296 | tf_op jit(solution)/shard_map/ppermute | solution.py:13
  42.1 1.0 copy-start.6
  47.2 69.6 %all-to-all-start.1 = ((bf16[64,2,1024]{2,1,0:T(2,128)(2,1)}), bf16[64,2,1024]{2,1,0:T(2,128)(2,1)S(1)}, u32[]{:S(2)}, u32[]{:S(2)}) async-start(bf16[64,2,1024]{2,1,0:T(2,128)(2,1)} %reshape.879), calls=%async_computation.1 | async-start | bytes 524288 | tf_op jit(solution)/shard_map/all_to_all | solution.py:200
  60.3 51.6 %copy-start.17 = (bf16[1,1024,128]{2,1,0:T(8,128)(2,1)S(1)}, bf16[1,1024,128]{2,1,0:T(8,128)(2,1)}, u32[]{:S(2)}) copy-start(bf16[1,1024,128]{2,1,0:T(8,128)(2,1)} %param.14) | copy-start | bytes 786436
  110.9 1.0 copy-start.8
  116.8 22.9 %all-to-all-start.3 = ((bf16[64,2,1024]{2,1,0:T(2,128)(2,1)}), bf16[64,2,1024]{2,1,0:T(2,128)(2,1)}, u32[]{:S(2)}, u32[]{:S(2)}) async-start(bf16[64,2,1024]{2,1,0:T(2,128)(2,1)} %reshape.883), calls=%async_computation.3 | async-start | bytes 524288 | tf_op jit(solution)/shard_map/all_to_all | solution.py:201
  130.3 1.1 copy-start.11
  133.2 26.6 %copy-start.1 = (f32[1,16,64,256]{3,2,1,0:T(8,128)}, f32[1,16,64,256]{3,2,1,0:T(8,128)S(1)}, u32[]{:S(2)}) copy-start(f32[1,16,64,256]{3,2,1,0:T(8,128)S(1)} %convolution_bitcast_fusion.2) | copy-start | bytes 3145732
  149.5 6.3 copy-start.3
  162.0 4.0 copy-start.2
  169.9 6.2 copy-start.14
  169.9 7.1 %copy-start.12 = (bf16[1024,1,128]{2,1,0:T(2,128)(2,1)S(1)}, bf16[1024,1,128]{2,1,0:T(2,128)(2,1)}, u32[]{:S(2)}) copy-start(bf16[1024,1,128]{2,1,0:T(2,128)(2,1)} %copy-done.11) | copy-start | bytes 786436
  194.4 60.0 %copy-start.10 = (f32[16,64,256]{2,1,0:T(8,128)S(1)}, f32[16,64,256]{2,1,0:T(8,128)}, u32[]{:S(2)}) copy-start(f32[16,64,256]{2,1,0:T(8,128)} %get-tuple-element.447) | copy-start | bytes 3145732
  245.9 85.7 %all-to-all-start.2 = ((bf16[64,2,1024]{2,1,0:T(2,128)(2,1)}), bf16[64,2,1024]{2,1,0:T(2,128)(2,1)S(1)}, u32[]{:S(2)}, u32[]{:S(2)}) async-start(bf16[64,2,1024]{2,1,0:T(2,128)(2,1)} %reshape.881), calls=%async_computation.2 | async-start | bytes 524288 | tf_op jit(solution)/shard_map/all_to_all | solution.py:214
  261.7 3.6 copy-start.15
  262.6 5.3 copy-start.16
  280.3 64.8 %copy-start = (f32[16,64,256]{2,1,0:T(8,128)S(1)}, f32[16,64,256]{2,1,0:T(8,128)}, u32[]{:S(2)}) copy-start(f32[16,64,256]{2,1,0:T(8,128)} %get-tuple-element.632) | copy-start | bytes 3145732
  280.3 64.8 %copy-start.35 = (f32[16,16]{1,0:T(8,128)S(1)}, f32[16,16]{1,0:T(8,128)}, u32[]{:S(2)}) copy-start(f32[16,16]{1,0:T(8,128)} %custom-call.2) | copy-start | bytes 3076
  280.3 64.8 %copy-start.36 = (f32[16,16]{1,0:T(8,128)S(1)}, f32[16,16]{1,0:T(8,128)}, u32[]{:S(2)}) copy-start(f32[16,16]{1,0:T(8,128)} %custom-call.3) | copy-start | bytes 3076
  331.6 156.5 %all-to-all-start.4 = ((bf16[64,2,1024]{2,1,0:T(2,128)(2,1)}), bf16[64,2,1024]{2,1,0:T(2,128)(2,1)}, u32[]{:S(2)}, u32[]{:S(2)}) async-start(bf16[64,2,1024]{2,1,0:T(2,128)(2,1)} %reshape.885), calls=%async_computation.4 | async-start | bytes 524288 | tf_op jit(solution)/shard_map/all_to_all | solution.py:215
  488.1 32.2 %all-to-all-start.5 = ((bf16[64,2,1024]{2,1,0:T(2,128)(2,1)}), bf16[64,2,1024]{2,1,0:T(2,128)(2,1)S(1)}, u32[]{:S(2)}, u32[]{:S(2)}) async-start(bf16[64,2,1024]{2,1,0:T(2,128)(2,1)} %reshape.887), calls=%async_computation.5 | async-start | bytes 524288 | tf_op jit(solution)/shard_map/all_to_all | solution.py:216
  501.5 18.0 %copy-start.5 = (f32[1,1024,130]{2,1,0:T(8,128)S(1)}, f32[1,1024,130]{2,1,0:T(8,128)}, u32[]{:S(2)}) copy-start(f32[1,1024,130]{2,1,0:T(8,128)} %copy-done.4) | copy-start | bytes 1597444
  520.3 15.9 %copy-start.7 = (f32[1,1024,130]{2,1,0:T(8,128)S(1)}, f32[1,1024,130]{2,1,0:T(8,128)}, u32[]{:S(2)}) copy-start(f32[1,1024,130]{2,1,0:T(8,128)} %copy-done.6) | copy-start | bytes 1597444
  528.0 9.1 %copy-start.9 = (f32[1,1024,130]{2,1,0:T(8,128)S(1)}, f32[1,1024,130]{2,1,0:T(8,128)}, u32[]{:S(2)}) copy-start(f32[1,1024,130]{2,1,0:T(8,128)} %copy-done.8) | copy-start | bytes 1597444
  528.0 9.1 %copy-start.18 = (bf16[1,1024,128]{2,1,0:T(8,128)(2,1)S(1)}, bf16[1,1024,128]{2,1,0:T(8,128)(2,1)}, u32[]{:S(2)}) copy-start(bf16[1,1024,128]{2,1,0:T(8,128)(2,1)} %param.14) | copy-start | bytes 786436
  536.0 96.0 %copy-start.28 = (f32[1,1,1024]{2,1,0:T(1,128)S(1)}, f32[1,1,1024]{2,1,0:T(1,128)}, u32[]{:S(2)}) copy-start(f32[1,1,1024]{2,1,0:T(1,128)} %copy-done.27) | copy-start | bytes 12292
  536.0 96.0 %copy-start.30 = (f32[1,1,1024]{2,1,0:T(1,128)S(1)}, f32[1,1,1024]{2,1,0:T(1,128)}, u32[]{:S(2)}) copy-start(f32[1,1,1024]{2,1,0:T(1,128)} %copy-done.29) | copy-start | bytes 12292
  536.0 96.0 %copy-start.32 = (f32[1,1,1024]{2,1,0:T(1,128)S(1)}, f32[1,1,1024]{2,1,0:T(1,128)}, u32[]{:S(2)}) copy-start(f32[1,1,1024]{2,1,0:T(1,128)} %copy-done.31) | copy-start | bytes 12292
  537.0 99.4 %copy-start.22 = (f32[1,1,1024]{2,1,0:T(1,128)S(1)}, f32[1,1,1024]{2,1,0:T(1,128)}, u32[]{:S(2)}) copy-start(f32[1,1,1024]{2,1,0:T(1,128)} %copy-done.21) | copy-start | bytes 12292
  537.1 99.4 %copy-start.24 = (f32[1,1,1024]{2,1,0:T(1,128)S(1)}, f32[1,1,1024]{2,1,0:T(1,128)}, u32[]{:S(2)}) copy-start(f32[1,1,1024]{2,1,0:T(1,128)} %copy-done.23) | copy-start | bytes 12292
  537.1 99.4 %copy-start.26 = (f32[1,1,1024]{2,1,0:T(1,128)S(1)}, f32[1,1,1024]{2,1,0:T(1,128)}, u32[]{:S(2)}) copy-start(f32[1,1,1024]{2,1,0:T(1,128)} %copy-done.25) | copy-start | bytes 12292
  615.1 16.8 %collective-permute-start.5 = (bf16[1,1024,2]{2,1,0:T(8,128)(2,1)S(1)}, bf16[1,1024,2]{2,1,0:T(8,128)(2,1)S(1)}, u32[]{:S(2)}, u32[]{:S(2)}) collective-permute-start(bf16[1,1024,2]{2,1,0:T(8,128)(2,1)S(1)} %bitcast.321), channel_id=1, source_target_pairs={{1,0},{2,1},{3,2},{4,3},{5,4},{6,5},{7,6},{8,7},{9,8},{10,9},{11,1... | collective-permute-start | bytes 12296 | tf_op jit(solution)/shard_map/ppermute | solution.py:13
  617.6 18.8 %collective-permute-start.4 = (bf16[1,1024,2]{2,1,0:T(8,128)(2,1)S(1)}, bf16[1,1024,2]{2,1,0:T(8,128)(2,1)S(1)}, u32[]{:S(2)}, u32[]{:S(2)}) collective-permute-start(bf16[1,1024,2]{2,1,0:T(8,128)(2,1)S(1)} %bitcast.318), channel_id=1, source_target_pairs={{1,0},{2,1},{3,2},{4,3},{5,4},{6,5},{7,6},{8,7},{9,8},{10,9},{11,1... | collective-permute-start | bytes 12296 | tf_op jit(solution)/shard_map/ppermute | solution.py:13
  621.1 16.9 %collective-permute-start.3 = (bf16[1,1024,2]{1,2,0:T(2,128)(2,1)S(1)}, bf16[1,1024,2]{1,2,0:T(2,128)(2,1)S(1)}, u32[]{:S(2)}, u32[]{:S(2)}) collective-permute-start(bf16[1,1024,2]{1,2,0:T(2,128)(2,1)S(1)} %copy.217), channel_id=1, source_target_pairs={{1,0},{2,1},{3,2},{4,3},{5,4},{6,5},{7,6},{8,7},{9,8},{10,9},{11,1... | collective-permute-start | bytes 12296 | tf_op jit(solution)/shard_map/ppermute | solution.py:13
  (1 other events, 0.9 us)
where the time goes:
time: 652 us; the launch traced here: 640 us
  other arithmetic  289 us (44%)
  local copies, waits for them, and re-layouts  99 us (15%)
  starting transfers between devices  91.3 us (14%)
  blocking collectives  85.8 us (13%)
  matrix products  48.9 us (8%)
  waiting for transfers between devices  22.9 us (4%)
    unnamed x9, other arithmetic  146 us
    psum x1, blocking collectives, per_device(): tap_total = lax.psum(tap_part, ('dp', 'context'))  75.4 us
    unnamed x93, local copies, waits for them, and re-layouts  48.6 us
    dot_general x16, matrix products, along_cols(): jnp.einsum('bckm,mj->bckj', array, table, precision=HIGHEST_PRECISION)  38.5 us
    reduce_sum x16, other arithmetic, one_mode(): jnp.sum(adj_re * tangents[0] + adj_im * tangents[1], axis=(1, 2))  35.3 us
    ppermute x6, waiting for transfers between devices, passed_along(): return lax.ppermute(x, axis, pairs)  18.1 us
    ppermute x6, starting transfers between devices, passed_along(): return lax.ppermute(x, axis, pairs)  18 us
    add x16, other arithmetic, add_mode(): carry[1] + weight_col * resp_im  16.5 us
  transfers between devices with their start and end apart: 12, of which 4 were waited for; matrix products, arithmetic and copies ran while one was open for 47% of the time, Pallas kernels for 0%

commit v1 on v0

--- a/solution.py
+++ b/solution.py
@@ -251,7 +251,9 @@
     token_scale = 1.0 / math.sqrt(
         queries.shape[0] * lax.axis_size("dp") * length_here * lax.axis_size("context")
     )
-    tap_total = lax.psum(tap_part, ("dp", "context"))
+    tap_total = tap_part
+    for mesh_axis in ("context", "dp"):
+        tap_total = lax.psum(tap_total, mesh_axis)
     residue_own, decay_own = lax.psum((residue_adj, decay_adj), "dp")
     return (
         output,

time: 652 us -> 948 us (1.45)
  blocking collectives: 85.8 us -> 362 us
  local copies, waits for them, and re-layouts: 99 us -> 115 us
    psum x2, blocking collectives: 85.8 us -> 362 us  [per_device(): tap_total = lax.psum(tap_total, mesh_axis)]
    dynamic_update_slice x32, local copies, waits for them, and re-layouts: 0.86 us -> 20.8 us  [mode_adjoints(): lax.scan(one_mode, jnp.zeros((), jnp.float32), (residues.T, decay_rates.T))]
    unnamed x93 -> x95, local copies, waits for them, and re-layouts: 48.6 us -> 45.1 us
  transfers between devices with their start and end apart: 12 -> 12, of which waited for: 4 -> 5; matrix products, arithmetic and copies ran while one was open for 47% -> 20% of each run, Pallas kernels for 0% -> 0%
where the time goes in v1:
time: 948 us; the launch traced here: 931 us
  blocking collectives  362 us (38%)
  other arithmetic  285 us (30%)
  local copies, waits for them, and re-layouts  115 us (12%)
  starting transfers between devices  86.9 us (9%)
  matrix products  51.7 us (5%)
  waiting for transfers between devices  26.4 us (3%)
    psum x2, blocking collectives, per_device(): tap_total = lax.psum(tap_total, mesh_axis)  362 us
    unnamed x9, other arithmetic  144 us
    unnamed x95, local copies, waits for them, and re-layouts  45.1 us
    dot_general x16, matrix products, along_cols(): jnp.einsum('bckm,mj->bckj', array, table, precision=HIGHEST_PRECISION)  41.5 us
    reduce_sum x16, other arithmetic, one_mode(): jnp.sum(adj_re * tangents[0] + adj_im * tangents[1], axis=(1, 2))  35.3 us
    dynamic_update_slice x32, local copies, waits for them, and re-layouts, mode_adjoints(): lax.scan(one_mode, jnp.zeros((), jnp.float32), (residues.T, decay_rates.T))  20.8 us
  transfers between devices with their start and end apart: 12, of which 5 were waited for; matrix products, arithmetic and copies ran while one was open for 20% of the time, Pallas kernels for 0%

profile of v1, /device:TPU:230, one launch (start us, length us, event | category | flops | bytes accessed | tf_op | source)
XLA Modules:
  0.0 930.6 jit_solution(18262843994272065466)
XLA Ops:
  4.7 7.0 collective-permute-done.1
  18.6 12.4 %all-to-all-start = ((bf16[64,2,1024]{2,1,0:T(2,128)(2,1)}), bf16[64,2,1024]{2,1,0:T(2,128)(2,1)S(1)}, u32[]{:S(2)}, u32[]{:S(2)}) async-start(bf16[64,2,1024]{2,1,0:T(2,128)(2,1)} %reshape.877), calls=%async_computation | async-start | bytes 524288 | tf_op jit(solution)/shard_map/all_to_all | solution.py:199
  31.9 4.9 collective-permute-start
  36.9 3.4 collective-permute-start.2
  41.7 3.5 collective-permute-done.2
  50.5 12.6 %all-to-all-start.1 = ((bf16[64,2,1024]{2,1,0:T(2,128)(2,1)}), bf16[64,2,1024]{2,1,0:T(2,128)(2,1)S(1)}, u32[]{:S(2)}, u32[]{:S(2)}) async-start(bf16[64,2,1024]{2,1,0:T(2,128)(2,1)} %reshape.879), calls=%async_computation.1 | async-start | bytes 524288 | tf_op jit(solution)/shard_map/all_to_all | solution.py:200
  63.1 48.0 %while.33 = (s32[]{:T(128)}, f32[16,64,256]{2,1,0:T(8,128)S(1)}, f32[16,64,256]{2,1,0:T(8,128)S(1)}, f32[16,16]{1,0:T(8,128)}, f32[16,16]{1,0:T(8,128)}, /*index=5*/s32[256]{0:T(256)S(1)}, s32[]{:T(128)}, s32[]{:T(128)}) while((s32[]{:T(128)}, f32[16,64,256]{2,1,0:T(8,128)S(1)}, ...), condition=%wide.region_1.2_spmd.clone.clone.clone, body=%wide.region_0.1_spmd.clone.clone.clone.sunk | while | flops 5062803 | bytes 4492591 | solution.py:113
  118.6 13.0 %all-to-all-start.3 = ((bf16[64,2,1024]{2,1,0:T(2,128)(2,1)}), bf16[64,2,1024]{2,1,0:T(2,128)(2,1)}, u32[]{:S(2)}, u32[]{:S(2)}) async-start(bf16[64,2,1024]{2,1,0:T(2,128)(2,1)} %reshape.883), calls=%async_computation.3 | async-start | bytes 524288 | tf_op jit(solution)/shard_map/all_to_all | solution.py:201
  133.7 7.8 all-to-all-done.3
  141.5 2.7 reshape.884
  148.0 3.1 convolution_bitcast_fusion.1
  160.4 2.2 fusion.62
  168.6 4.7 multiply_add_fusion.3
  173.3 2.9 fusion.77
  176.3 3.0 fusion.132
  179.3 88.0 %while.32 = (s32[]{:T(128)}, f32[16,16]{1,0:T(8,128)S(1)}, f32[16,16]{1,0:T(8,128)}, f32[16,16]{1,0:T(8,128)}, f32[16,64,256]{2,1,0:T(8,128)S(1)}, /*index=5*/f3...) while((s32[]{:T(128)}, f32[16,16]{1,0:T(8,128)S(1)}, ...), condition=%wide.region_16.17_spmd.clone.clone.clone, body=%wide.region_13.16_spmd.clone.clone.clone.sunk | while | flops 12403026 | bytes 2396669 | solution.py:136
  186.1 2.2 fusion.310
  240.7 2.2 fusion.310
  267.2 3.2 convolution_add_fusion
  270.4 3.3 convolution_add_fusion.1
  275.6 3.0 fusion.136
  278.7 2.6 copy.231
  281.3 2.6 copy.221
  283.9 2.6 copy.225
  286.5 9.7 %multiply_convert_fusion = (bf16[1,16,8192]{1,0,2:T(2,128)(2,1)}, bf16[1,16,8192]{1,0,2:T(2,128)(2,1)}) fusion(f32[1,16,8192]{1,0,2:T(1,128)} %bitcast.306, f32[1,16,8192]{1,0,2:T(1,128)} %bitcast.308, f32[1,16,8192]{1,0,2:T(1,128)} %bitcast.307), kind=kLoop, calls=%fused_computation.90 | loop fusion | flops 524288 | bytes 2097152 | tf_op jit(solution)/shard_map/convert_element_type | solution.py:210
  296.2 45.4 %reduce.5 = bf16[8192,16]{1,0:T(8,128)(2,1)S(1)} reduce(bf16[8192,1,16]{2,1,0:T(2,128)(2,1)} %bitcast.309, bf16[]{:T(256)} %broadcast.596), dimensions={1}, to_apply=%bitcast.259.reduce_sub_computation | reduce | bytes 524290
  341.6 2.9 reshape.887
  344.5 46.8 %reduce.4 = bf16[8192,16]{1,0:T(8,128)(2,1)} reduce(bf16[8192,1,16]{2,1,0:T(2,128)(2,1)} %bitcast.305, bf16[]{:T(256)} %broadcast.596), dimensions={1}, to_apply=%bitcast.257.reduce_sub_computation | reduce | bytes 524290
  391.4 4.4 reshape.885
  395.7 8.2 all-to-all-start.5
  403.9 3.2 convolution_add_fusion.4
  411.1 2.8 all-to-all-done.5
  414.6 10.5 %all-to-all-start.4 = ((bf16[64,2,1024]{2,1,0:T(2,128)(2,1)}), bf16[64,2,1024]{2,1,0:T(2,128)(2,1)S(1)}, u32[]{:S(2)}, u32[]{:S(2)}) async-start(bf16[64,2,1024]{2,1,0:T(2,128)(2,1)} %reshape.885), calls=%async_computation.4 | async-start | bytes 524288 | tf_op jit(solution)/shard_map/all_to_all | solution.py:215
  429.8 6.7 copy.214
  436.5 45.2 %reduce.3 = bf16[8192,16]{1,0:T(8,128)(2,1)S(1)} reduce(bf16[8192,1,16]{2,1,0:T(2,128)(2,1)} %bitcast.310, bf16[]{:T(256)} %broadcast.596), dimensions={1}, to_apply=%bitcast.253.reduce_sub_computation | reduce | bytes 524290
  481.7 2.9 reshape.881
  484.6 7.6 reshape.888
  492.2 7.9 copy.227
  500.4 2.8 collective-permute-start.5
  503.1 12.5 %all-to-all-start.2 = ((bf16[64,2,1024]{2,1,0:T(2,128)(2,1)}), bf16[64,2,1024]{2,1,0:T(2,128)(2,1)S(1)}, u32[]{:S(2)}, u32[]{:S(2)}) async-start(bf16[64,2,1024]{2,1,0:T(2,128)(2,1)} %reshape.881), calls=%async_computation.2 | async-start | bytes 524288 | tf_op jit(solution)/shard_map/all_to_all | solution.py:214
  515.7 7.6 reshape.886
  523.3 8.0 copy.223
  531.5 2.9 collective-permute-start.4
  536.0 7.6 reshape.882
  543.6 8.0 copy.215
  553.7 350.7 %psum.28 = f32[3,3,1024]{2,1,0:T(4,128)S(1)} all-reduce(f32[3,3,1024]{2,1,0:T(4,128)S(1)} %pad_maximum_fusion), channel_id=1, replica_groups=mesh['dp'=4,'context'=64] {'context'}, use_global_device_ids=true, to_apply=%region_11.12 | all-reduce | flops 9216 | bytes 73728 | tf_op jit(solution)/shard_map/psum | solution.py:256
  904.4 11.1 %all-reduce = (f32[3,3,1024]{2,1,0:T(4,128)S(1)}, f32[16,16]{1,0:T(8,128)S(1)}, f32[16,16]{1,0:T(8,128)S(1)}) all-reduce(f32[3,3,1024]{2,1,0:T(4,128)S(1)} %psum.28, f32[16,16]{1,0:T(8,128)S(1)} %bitcast.356, f32[16,16]{1,0:T(8,128)S(1)} %bitcast.355), channel_id=1, replica_groups=mesh['dp'=4,'context'=64] {'dp'}, use_global_device_ids=true, to_apply=%region_12.13 | all-reduce | flops 9728 | bytes 77824 | tf_op jit(solution)/shard_map/psum | solution.py:256
  923.5 5.2 collective-permute-done.3
  (408 shorter events, 201.6 us)
Async XLA Ops:
  0.6 30.4 %copy-start.19 = (bf16[1,1024,128]{2,1,0:T(8,128)(2,1)S(1)}, bf16[1,1024,128]{2,1,0:T(8,128)(2,1)}, u32[]{:S(2)}) copy-start(bf16[1,1024,128]{2,1,0:T(8,128)(2,1)} %param.11) | copy-start | bytes 786436
  0.6 36.1 %copy-start.18 = (bf16[1,1024,128]{2,1,0:T(8,128)(2,1)S(1)}, bf16[1,1024,128]{2,1,0:T(8,128)(2,1)}, u32[]{:S(2)}) copy-start(bf16[1,1024,128]{2,1,0:T(8,128)(2,1)} %param.13) | copy-start | bytes 786436
  0.7 39.7 %copy-start.34 = (f32[16,16]{1,0:T(8,128)S(1)}, f32[16,16]{1,0:T(8,128)}, u32[]{:S(2)}) copy-start(f32[16,16]{1,0:T(8,128)} %param.16) | copy-start | bytes 3076
  0.7 40.3 %copy-start.35 = (f32[16,16]{1,0:T(8,128)S(1)}, f32[16,16]{1,0:T(8,128)}, u32[]{:S(2)}) copy-start(f32[16,16]{1,0:T(8,128)} %param.17) | copy-start | bytes 3076
  1.8 9.9 %collective-permute-start.1 = (bf16[1,1024,2]{2,1,0:T(8,128)(2,1)S(1)}, bf16[1,1024,2]{2,1,0:T(8,128)(2,1)S(1)}, u32[]{:S(2)}, u32[]{:S(2)}) collective-permute-start(bf16[1,1024,2]{2,1,0:T(8,128)(2,1)S(1)} %slice.146), channel_id=1, source_target_pairs={{0,1},{1,2},{2,3},{3,4},{4,5},{5,6},{6,7},{7,8},{8,9},{9,10},{10,1... | collective-permute-start | bytes 12296 | tf_op jit(solution)/shard_map/ppermute | solution.py:13
  4.7 13.9 %copy-start.20 = (f32[1,1,1024]{2,1,0:T(1,128)}, f32[1,1,1024]{2,1,0:T(1,128)S(1)}, u32[]{:S(2)}) copy-start(f32[1,1,1024]{2,1,0:T(1,128)S(1)} %get-tuple-element.453) | copy-start | bytes 12292
  4.7 13.9 %copy-start.22 = (f32[1,1,1024]{2,1,0:T(1,128)}, f32[1,1,1024]{2,1,0:T(1,128)S(1)}, u32[]{:S(2)}) copy-start(f32[1,1,1024]{2,1,0:T(1,128)S(1)} %get-tuple-element.454) | copy-start | bytes 12292
  4.7 13.9 %copy-start.24 = (f32[1,1,1024]{2,1,0:T(1,128)}, f32[1,1,1024]{2,1,0:T(1,128)S(1)}, u32[]{:S(2)}) copy-start(f32[1,1,1024]{2,1,0:T(1,128)S(1)} %get-tuple-element.455) | copy-start | bytes 12292
  4.7 40.7 %copy-start.26 = (f32[1,1,1024]{2,1,0:T(1,128)}, f32[1,1,1024]{2,1,0:T(1,128)S(1)}, u32[]{:S(2)}) copy-start(f32[1,1,1024]{2,1,0:T(1,128)S(1)} %get-tuple-element.452) | copy-start | bytes 12292
  4.7 40.7 %copy-start.28 = (f32[1,1,1024]{2,1,0:T(1,128)}, f32[1,1,1024]{2,1,0:T(1,128)S(1)}, u32[]{:S(2)}) copy-start(f32[1,1,1024]{2,1,0:T(1,128)S(1)} %get-tuple-element.459) | copy-start | bytes 12292
  4.7 40.7 %copy-start.30 = (f32[1,1,1024]{2,1,0:T(1,128)}, f32[1,1,1024]{2,1,0:T(1,128)S(1)}, u32[]{:S(2)}) copy-start(f32[1,1,1024]{2,1,0:T(1,128)S(1)} %get-tuple-element.460) | copy-start | bytes 12292
  18.6 31.9 %all-to-all-start = ((bf16[64,2,1024]{2,1,0:T(2,128)(2,1)}), bf16[64,2,1024]{2,1,0:T(2,128)(2,1)S(1)}, u32[]{:S(2)}, u32[]{:S(2)}) async-start(bf16[64,2,1024]{2,1,0:T(2,128)(2,1)} %reshape.877), calls=%async_computation | async-start | bytes 524288 | tf_op jit(solution)/shard_map/all_to_all | solution.py:199
  31.9 79.5 %collective-permute-start = (bf16[1,1024,2]{1,2,0:T(2,128)(2,1)}, bf16[1,1024,2]{1,2,0:T(2,128)(2,1)}, u32[]{:S(2)}, u32[]{:S(2)}) collective-permute-start(bf16[1,1024,2]{1,2,0:T(2,128)(2,1)} %copy.232), channel_id=1, source_target_pairs={{0,1},{1,2},{2,3},{3,4},{4,5},{5,6},{6,7},{7,8},{8,9},{9,10},{10,1... | collective-permute-start | bytes 12296 | tf_op jit(solution)/shard_map/ppermute | solution.py:13
  36.9 8.3 collective-permute-start.2
  45.4 1.0 copy-start.4
  50.5 68.1 %all-to-all-start.1 = ((bf16[64,2,1024]{2,1,0:T(2,128)(2,1)}), bf16[64,2,1024]{2,1,0:T(2,128)(2,1)S(1)}, u32[]{:S(2)}, u32[]{:S(2)}) async-start(bf16[64,2,1024]{2,1,0:T(2,128)(2,1)} %reshape.879), calls=%async_computation.1 | async-start | bytes 524288 | tf_op jit(solution)/shard_map/all_to_all | solution.py:200
  63.1 50.4 %copy-start.13 = (bf16[1,1024,128]{2,1,0:T(8,128)(2,1)S(1)}, bf16[1,1024,128]{2,1,0:T(8,128)(2,1)}, u32[]{:S(2)}) copy-start(bf16[1,1024,128]{2,1,0:T(8,128)(2,1)} %param.14) | copy-start | bytes 786436
  112.5 1.0 copy-start.6
  118.6 22.9 %all-to-all-start.3 = ((bf16[64,2,1024]{2,1,0:T(2,128)(2,1)}), bf16[64,2,1024]{2,1,0:T(2,128)(2,1)}, u32[]{:S(2)}, u32[]{:S(2)}) async-start(bf16[64,2,1024]{2,1,0:T(2,128)(2,1)} %reshape.883), calls=%async_computation.3 | async-start | bytes 524288 | tf_op jit(solution)/shard_map/all_to_all | solution.py:201
  153.6 4.7 copy-start.1
  173.3 5.9 copy-start
  173.3 5.9 copy-start.36
  179.3 88.0 %copy-start.8 = (f32[16,64,256]{2,1,0:T(8,128)S(1)}, f32[16,64,256]{2,1,0:T(8,128)}, u32[]{:S(2)}) copy-start(f32[16,64,256]{2,1,0:T(8,128)} %get-tuple-element.448) | copy-start | bytes 3145732
  267.2 7.4 copy-start.37
  270.4 5.2 copy-start.9
  275.6 5.7 copy-start.12
  278.6 5.3 copy-start.11
  344.5 59.4 %copy-start.10 = (f32[16,64,256]{2,1,0:T(8,128)S(1)}, f32[16,64,256]{2,1,0:T(8,128)}, u32[]{:S(2)}) copy-start(f32[16,64,256]{2,1,0:T(8,128)} %get-tuple-element.450) | copy-start | bytes 3145732
  395.7 18.1 %all-to-all-start.5 = ((bf16[64,2,1024]{2,1,0:T(2,128)(2,1)}), bf16[64,2,1024]{2,1,0:T(2,128)(2,1)S(1)}, u32[]{:S(2)}, u32[]{:S(2)}) async-start(bf16[64,2,1024]{2,1,0:T(2,128)(2,1)} %reshape.887), calls=%async_computation.5 | async-start | bytes 524288 | tf_op jit(solution)/shard_map/all_to_all | solution.py:216
  414.6 88.5 %all-to-all-start.4 = ((bf16[64,2,1024]{2,1,0:T(2,128)(2,1)}), bf16[64,2,1024]{2,1,0:T(2,128)(2,1)S(1)}, u32[]{:S(2)}, u32[]{:S(2)}) async-start(bf16[64,2,1024]{2,1,0:T(2,128)(2,1)} %reshape.885), calls=%async_computation.4 | async-start | bytes 524288 | tf_op jit(solution)/shard_map/all_to_all | solution.py:215
  436.4 48.2 %copy-start.17 = (bf16[64,2,1024]{2,1,0:T(2,128)(2,1)S(1)}, bf16[64,2,1024]{2,1,0:T(2,128)(2,1)}, u32[]{:S(2)}) copy-start(bf16[64,2,1024]{2,1,0:T(2,128)(2,1)} %copy-done.16) | copy-start | bytes 786436
  500.4 419.0 %collective-permute-start.5 = (bf16[1,1024,2]{2,1,0:T(8,128)(2,1)S(1)}, bf16[1,1024,2]{2,1,0:T(8,128)(2,1)}, u32[]{:S(2)}, u32[]{:S(2)}) collective-permute-start(bf16[1,1024,2]{2,1,0:T(8,128)(2,1)S(1)} %bitcast.318), channel_id=1, source_target_pairs={{1,0},{2,1},{3,2},{4,3},{5,4},{6,5},{7,6},{8,7},{9,8},{10,9},{11,1... | collective-permute-start | bytes 12296 | tf_op jit(solution)/shard_map/ppermute | solution.py:13
  503.1 32.9 %all-to-all-start.2 = ((bf16[64,2,1024]{2,1,0:T(2,128)(2,1)}), bf16[64,2,1024]{2,1,0:T(2,128)(2,1)S(1)}, u32[]{:S(2)}, u32[]{:S(2)}) async-start(bf16[64,2,1024]{2,1,0:T(2,128)(2,1)} %reshape.881), calls=%async_computation.2 | async-start | bytes 524288 | tf_op jit(solution)/shard_map/all_to_all | solution.py:214
  515.7 18.8 %copy-start.5 = (f32[1,1024,130]{2,1,0:T(8,128)S(1)}, f32[1,1024,130]{2,1,0:T(8,128)}, u32[]{:S(2)}) copy-start(f32[1,1024,130]{2,1,0:T(8,128)} %copy-done.4) | copy-start | bytes 1597444
  523.3 11.9 %copy-start.3 = (f32[1,1024,130]{2,1,0:T(8,128)S(1)}, f32[1,1024,130]{2,1,0:T(8,128)}, u32[]{:S(2)}) copy-start(f32[1,1024,130]{2,1,0:T(8,128)} %copy-done.2) | copy-start | bytes 1597444
  531.5 390.4 %collective-permute-start.4 = (bf16[1,1024,2]{2,1,0:T(8,128)(2,1)S(1)}, bf16[1,1024,2]{2,1,0:T(8,128)(2,1)S(1)}, u32[]{:S(2)}, u32[]{:S(2)}) collective-permute-start(bf16[1,1024,2]{2,1,0:T(8,128)(2,1)S(1)} %bitcast.320), channel_id=1, source_target_pairs={{1,0},{2,1},{3,2},{4,3},{5,4},{6,5},{7,6},{8,7},{9,8},{10,9},{11,1... | collective-permute-start | bytes 12296 | tf_op jit(solution)/shard_map/ppermute | solution.py:13
  543.6 8.5 copy-start.7
  543.6 8.5 copy-start.14
  543.6 8.5 copy-start.15
  551.6 352.7 %copy-start.32 = (f32[16,16]{0,1:T(8,128)S(1)}, f32[16,16]{0,1:T(8,128)}, u32[]{:S(2)}) copy-start(f32[16,16]{0,1:T(8,128)} %copy.230) | copy-start | bytes 3076
  551.6 352.7 %copy-start.33 = (f32[16,16]{0,1:T(8,128)S(1)}, f32[16,16]{0,1:T(8,128)}, u32[]{:S(2)}) copy-start(f32[16,16]{0,1:T(8,128)} %copy.229) | copy-start | bytes 3076
  551.7 368.8 %copy-start.27 = (f32[1,1,1024]{2,1,0:T(1,128)S(1)}, f32[1,1,1024]{2,1,0:T(1,128)}, u32[]{:S(2)}) copy-start(f32[1,1,1024]{2,1,0:T(1,128)} %copy-done.26) | copy-start | bytes 12292
  551.7 368.8 %copy-start.29 = (f32[1,1,1024]{2,1,0:T(1,128)S(1)}, f32[1,1,1024]{2,1,0:T(1,128)}, u32[]{:S(2)}) copy-start(f32[1,1,1024]{2,1,0:T(1,128)} %copy-done.28) | copy-start | bytes 12292
  551.7 368.8 %copy-start.31 = (f32[1,1,1024]{2,1,0:T(1,128)S(1)}, f32[1,1,1024]{2,1,0:T(1,128)}, u32[]{:S(2)}) copy-start(f32[1,1,1024]{2,1,0:T(1,128)} %copy-done.30) | copy-start | bytes 12292
  552.2 369.8 %copy-start.21 = (f32[1,1,1024]{2,1,0:T(1,128)S(1)}, f32[1,1,1024]{2,1,0:T(1,128)}, u32[]{:S(2)}) copy-start(f32[1,1,1024]{2,1,0:T(1,128)} %copy-done.20) | copy-start | bytes 12292
  552.2 369.8 %copy-start.23 = (f32[1,1,1024]{2,1,0:T(1,128)S(1)}, f32[1,1,1024]{2,1,0:T(1,128)}, u32[]{:S(2)}) copy-start(f32[1,1,1024]{2,1,0:T(1,128)} %copy-done.22) | copy-start | bytes 12292
  552.2 369.8 %copy-start.25 = (f32[1,1,1024]{2,1,0:T(1,128)S(1)}, f32[1,1,1024]{2,1,0:T(1,128)}, u32[]{:S(2)}) copy-start(f32[1,1,1024]{2,1,0:T(1,128)} %copy-done.24) | copy-start | bytes 12292
  917.5 11.2 %collective-permute-start.3 = (bf16[1,1024,2]{1,2,0:T(2,128)(2,1)S(1)}, bf16[1,1024,2]{1,2,0:T(2,128)(2,1)S(1)}, u32[]{:S(2)}, u32[]{:S(2)}) collective-permute-start(bf16[1,1024,2]{1,2,0:T(2,128)(2,1)S(1)} %copy.217), channel_id=1, source_target_pairs={{1,0},{2,1},{3,2},{4,3},{5,4},{6,5},{7,6},{8,7},{9,8},{10,9},{11,1... | collective-permute-start | bytes 12296 | tf_op jit(solution)/shard_map/ppermute | solution.py:13
  (2 other events, 1.7 us)
